TPU v7x, 128 devices: a whole 4x4x4 slice. The times are simulated.
128 devices in a mesh: bath: 32 (over x, y, z_hi), imp: 4 (over z_lo, core).
Axes of the slice: x: 4, y: 4, z: 4 (z_hi: 2, z_lo: 2; z = z_hi * 2 + z_lo), core: 2. Of those that a mesh axis runs over, the one named last changes fastest.
Arguments:
- psi: bfloat16 [32, 1024, 2048], P('bath', 'imp'), may hold values from -6 to 6
- h_imp: bfloat16 [1024, 1024], P(None, 'imp'), may hold values from -0.1875 to 0.1875
- hops: bfloat16 [2, 5, 1024, 1024], P(None, None, None, 'imp'), may hold values from -0.3125 to 0.3125
- patterns: int32 [2, 5, 8, 8], replicated, may hold values from 0 to 1, as said below
- signs: int32 [5, 32, 8], P(None, 'bath'), may hold values 0 or 1
- bath_energy: float32 [32], P('bath'), may hold values from -2 to 2
Outputs:
- applied: float32 [32, 1024, 2048], P('bath', 'imp')
Inputs may be any that keep to these rules, and one draw needn't show every extreme that they name: `patterns`: each hybridization operator has exactly 24 nonzero blocks.
All inputs are finite; a program needn't handle non-finite values. No bound on the sum of `signs` on one device may be relied on, other than what follows from the above.
Results may differ from a plain program's by a relative error of at most 0.0003.
Values may be sent and summed in bfloat16 or wider, within the bound.
A program may use at most 128 MiB of HBM per device.

v0:
```python
import jax
import jax.numpy as jnp
from jax import lax
from jax.sharding import PartitionSpec as P


def partner_2(value, axis, stride):
    return lax.ppermute(value, axis, [(i, i ^ 1 << stride) for i in range(lax.axis_size(axis))])


def per_device(psi, h_imp, hops, patterns, signs, bath_energy):
    local = psi[0]
    rows_dev = local.shape[0]
    imps = h_imp.shape[0]
    levels = hops.shape[1]
    nblocks = patterns.shape[2]
    blk = imps // nblocks
    dev_blocks = rows_dev // blk
    col_index = lax.axis_index("imp")
    bath_index = lax.axis_index("bath")
    partners = []
    sides = []
    for level in range(levels):
        partners.append(partner_2(local, "bath", level))
        sides.append(jnp.bitwise_and(jnp.right_shift(bath_index, level), 1))
    gathered = []
    for level in range(levels):
        columns = lax.dynamic_slice_in_dim(
            jnp.where(sides[level] == 1, patterns[1, level], patterns[0, level]),
            col_index * dev_blocks,
            dev_blocks,
            1,
        )
        full_mask = jnp.repeat(jnp.repeat(columns, blk, axis=0), blk, axis=1).astype(jnp.bfloat16)
        gathered.append(
            (
                jnp.where(sides[level] == 1, hops[1, level], hops[0, level]) * full_mask,
                jnp.repeat(1.0 - 2.0 * signs[level, 0].astype(jnp.float32), blk),
                partners[level],
            )
        )
    total = jnp.zeros((rows_dev * lax.axis_size("imp"), local.shape[1]), jnp.float32)
    for matrix, factor, partner in gathered:
        total = total + factor[:, None] * jnp.dot(
            matrix, partner, preferred_element_type=jnp.float32
        )
    summed = lax.psum_scatter(
        jnp.dot(h_imp, local, preferred_element_type=jnp.float32) + total,
        "imp",
        scatter_dimension=0,
        tiled=True,
    )
    applied = summed + bath_energy[0] * local.astype(jnp.float32)
    return applied[None]


def solution(mesh):
    placed = (
        P("bath", "imp", None),
        P(None, "imp"),
        P(None, None, None, "imp"),
        P(),
        P(None, "bath", None),
        P("bath"),
    )
    return jax.shard_map(
        per_device, mesh=mesh, in_specs=placed, out_specs=P("bath", "imp", None), check_vma=False
    )
```

profile of v0, /device:TPU:1, one launch (start us, length us, event | category | flops | bytes accessed | tf_op | source)
XLA Modules:
  0.0 186.1 jit_solution(15221122158810702896)
XLA Ops:
  6.5 2.0 %collective-permute-start.3 = (bf16[256,2048]{1,0:T(8,128)(2,1)}, bf16[256,2048]{1,0:T(8,128)(2,1)}, u32[]{:S(2)}, u32[]{:S(2)}) collective-permute-start(bf16[256,2048]{1,0:T(8,128)(2,1)} %bitcast.94), channel_id=1, source_target_pairs={{0,32},{4,36},{8,40},{12,44},{16,48},{20,52},{24,56},{28,60},{32,0... | collective-permute-start | bytes 3145736 | tf_op jit(solution)/shard_map/ppermute | solution.py:8
  8.6 2.9 %collective-permute-start.2 = (bf16[256,2048]{1,0:T(8,128)(2,1)}, bf16[256,2048]{1,0:T(8,128)(2,1)}, u32[]{:S(2)}, u32[]{:S(2)}) collective-permute-start(bf16[256,2048]{1,0:T(8,128)(2,1)} %bitcast.95), channel_id=1, source_target_pairs={{0,16},{4,20},{8,24},{12,28},{16,0},{20,4},{24,8},{28,12},{32,48},... | collective-permute-start | bytes 3145736 | tf_op jit(solution)/shard_map/ppermute | solution.py:8
  11.5 0.4 collective-permute-start.1
  11.9 3.6 %collective-permute-start = (bf16[256,2048]{1,0:T(8,128)(2,1)}, bf16[256,2048]{1,0:T(8,128)(2,1)S(1)}, u32[]{:S(2)}, u32[]{:S(2)}) collective-permute-start(bf16[256,2048]{1,0:T(8,128)(2,1)} %bitcast.97), channel_id=1, source_target_pairs={{0,4},{4,0},{8,12},{12,8},{16,20},{20,16},{24,28},{28,24},{32,36},... | collective-permute-start | bytes 3145736 | tf_op jit(solution)/shard_map/ppermute | solution.py:8
  15.5 2.5 %collective-permute-start.4 = (bf16[256,2048]{1,0:T(8,128)(2,1)}, bf16[256,2048]{1,0:T(8,128)(2,1)}, u32[]{:S(2)}, u32[]{:S(2)}) collective-permute-start(bf16[256,2048]{1,0:T(8,128)(2,1)} %bitcast.98), channel_id=1, source_target_pairs={{0,64},{4,68},{8,72},{12,76},{16,80},{20,84},{24,88},{28,92},{32,9... | collective-permute-start | bytes 3145736 | tf_op jit(solution)/shard_map/ppermute | solution.py:8
  17.9 0.7 subtract_bitcast_fusion.4
  18.7 0.1 broadcast_bitcast_fusion.4
  18.7 0.8 slice_select_fusion
  19.6 0.1 fusion.36
  19.6 0.1 fusion.34
  19.7 0.1 broadcast_bitcast_fusion
  19.8 0.1 broadcast_bitcast_fusion.2
  19.9 5.9 %fusion.39 = f32[1024,2048]{1,0:T(8,128)} fusion(bf16[1024,256]{1,0:T(8,128)(2,1)S(1)} %copy-done, bf16[1,256,2048]{2,1,0:T(8,128)(2,1)} %param.6), kind=kOutput, calls=%fused_computation.66 | convolution fusion | flops 1073741824 | bytes 9961472 | tf_op jit(solution)/shard_map/dot_general | solution.py:48
  25.7 0.1 fusion.38
  25.8 5.5 %collective-permute-done.3 = bf16[256,2048]{1,0:T(8,128)(2,1)} collective-permute-done((bf16[256,2048]{1,0:T(8,128)(2,1)}, bf16[256,2048]{1,0:T(8,128)(2,1)}, u32[]{:S(2)}, u32[]{:S(2)}) %collective-permute-start.3) | collective-permute-done | bytes 1048608 | tf_op jit(solution)/shard_map/ppermute | solution.py:8
  31.3 2.9 %broadcast_in_dim.59 = bf16[1024,2,128]{2,1,0:T(2,128)(2,1)S(1)} broadcast(bf16[1024,2]{1,0:T(8,128)(2,1)S(1)} %bitcast.106), dimensions={0,1} | broadcast | bytes 528384 | tf_op jit(solution)/shard_map/broadcast_in_dim | solution.py:34
  34.3 5.7 %fusion.1 = f32[1024,2048]{1,0:T(8,128)} fusion(bf16[256,2048]{1,0:T(8,128)(2,1)} %collective-permute-done.3, bf16[128,8,2,128]{3,2,1,0:T(2,128)(2,1)S(1)} %bitcast.99, bf16[2,5,1024,256]{3,2,1,0:T(8,128)(2,1)S(1)} %bitcast.105, pred[]{:T(512)S(6)} %eq.23), kind=kOutput, calls=%fused_computation.5 | convolution fusion | flops 1074266112 | bytes 11010049 | tf_op jit(solution)/shard_map/dot_general | solution.py:44
  40.0 0.0 collective-permute-done.2
  40.1 2.9 %broadcast_in_dim.56 = bf16[1024,2,128]{2,1,0:T(2,128)(2,1)S(1)} broadcast(bf16[1024,2]{1,0:T(8,128)(2,1)S(1)} %bitcast.107), dimensions={0,1} | broadcast | bytes 528384 | tf_op jit(solution)/shard_map/broadcast_in_dim | solution.py:34
  43.0 5.7 %fusion.3 = f32[1024,2048]{1,0:T(8,128)} fusion(bf16[256,2048]{1,0:T(8,128)(2,1)} %collective-permute-done.2, bf16[128,8,2,128]{3,2,1,0:T(2,128)(2,1)S(1)} %bitcast.100, bf16[2,5,1024,256]{3,2,1,0:T(8,128)(2,1)S(1)} %bitcast.105, pred[]{:T(512)S(6)} %eq.22), kind=kOutput, calls=%fused_computation.8 | convolution fusion | flops 1074266112 | bytes 11010049 | tf_op jit(solution)/shard_map/dot_general | solution.py:44
  48.7 8.2 %collective-permute-done.1 = bf16[256,2048]{1,0:T(8,128)(2,1)} collective-permute-done((bf16[256,2048]{1,0:T(8,128)(2,1)}, bf16[256,2048]{1,0:T(8,128)(2,1)}, u32[]{:S(2)}, u32[]{:S(2)}) %collective-permute-start.1) | collective-permute-done | bytes 1048608 | tf_op jit(solution)/shard_map/ppermute | solution.py:8
  57.0 2.9 %broadcast_in_dim.53 = bf16[1024,2,128]{2,1,0:T(2,128)(2,1)S(1)} broadcast(bf16[1024,2]{1,0:T(8,128)(2,1)S(1)} %bitcast.108), dimensions={0,1} | broadcast | bytes 528384 | tf_op jit(solution)/shard_map/broadcast_in_dim | solution.py:34
  59.9 5.7 %fusion.5 = f32[1024,2048]{1,0:T(8,128)} fusion(bf16[256,2048]{1,0:T(8,128)(2,1)} %collective-permute-done.1, bf16[128,8,2,128]{3,2,1,0:T(2,128)(2,1)S(1)} %bitcast.101, bf16[2,5,1024,256]{3,2,1,0:T(8,128)(2,1)S(1)} %bitcast.105, pred[]{:T(512)S(6)} %eq.21), kind=kOutput, calls=%fused_computation.11 | convolution fusion | flops 1074266112 | bytes 11010049 | tf_op jit(solution)/shard_map/dot_general | solution.py:44
  65.6 0.0 collective-permute-done
  65.7 2.9 %broadcast_in_dim.50 = bf16[1024,2,128]{2,1,0:T(2,128)(2,1)S(1)} broadcast(bf16[1024,2]{1,0:T(8,128)(2,1)S(1)} %bitcast.109), dimensions={0,1} | broadcast | bytes 528384 | tf_op jit(solution)/shard_map/broadcast_in_dim | solution.py:34
  68.6 4.5 %fusion.7 = f32[1024,2048]{1,0:T(8,128)} fusion(bf16[256,2048]{1,0:T(8,128)(2,1)S(1)} %collective-permute-done, bf16[128,8,2,128]{3,2,1,0:T(2,128)(2,1)S(1)} %bitcast.102, bf16[2,5,1024,256]{3,2,1,0:T(8,128)(2,1)S(1)} %bitcast.105, pred[]{:T(512)S(6)} %eq.20), kind=kOutput, calls=%fused_computation.14 | convolution fusion | flops 1074266112 | bytes 11010049 | tf_op jit(solution)/shard_map/dot_general | solution.py:44
  73.2 2.9 %broadcast_in_dim.62 = bf16[1024,2,128]{2,1,0:T(2,128)(2,1)S(1)} broadcast(bf16[1024,2]{1,0:T(8,128)(2,1)S(1)} %bitcast.110), dimensions={0,1} | broadcast | bytes 528384 | tf_op jit(solution)/shard_map/broadcast_in_dim | solution.py:34
  76.1 0.0 copy-start.1
  76.1 18.4 %add_add_fusion = f32[1024,2048]{1,0:T(8,128)} fusion(f32[1024,2048]{1,0:T(8,128)} %fusion.39, f32[1024,2048]{1,0:T(8,128)} %fusion.1, f32[1024,2048]{1,0:T(8,128)} %fusion.3, f32[1024,2048]{1,0:T(8,128)} %fusion.5, f32[1024,2048]{1,0:T(8,128)} %fusion.7, bf16[256,2048]{1,0:T(8,128)(2,1)} %collective-permute-done.4, f32[1024]{0:T(1024)S(1)} %get-tuple-element.19, ...), kind=kOutput, calls=%fused_computation | convolution fusion | flops 1095237632 | bytes 52973568 | tf_op jit(solution)/shard_map/dot_general | solution.py:44
  94.5 0.0 reduce-scatter.2.cloned.1.call-update
  95.2 80.7 %reduce-scatter.2.cloned.1.call-done = f32[256,2048]{1,0:T(8,128)} async-done(((f32[1024,2048]{1,0:T(8,128)}), f32[256,2048]{1,0:T(8,128)}) %reduce-scatter.2.cloned.1.call-update) | async-done | bytes 2097168 | tf_op jit(solution)/shard_map/reduce_scatter | solution.py:47
  176.0 3.3 %add_bitcast_fusion = f32[1,256,2048]{2,1,0:T(8,128)} fusion(f32[256,2048]{1,0:T(8,128)} %reduce-scatter.2.cloned.1.call-done, f32[]{:T(128)} %bitcast.93, bf16[1,256,2048]{2,1,0:T(8,128)(2,1)S(1)} %copy-done.2), kind=kLoop, calls=%fused_computation.1 | loop fusion | flops 1572864 | bytes 5242884 | tf_op jit(solution)/shard_map/broadcast_in_dim | solution.py:54
  (17 shorter events, 0.2 us)
Async XLA Ops:
  6.5 13.3 %copy-start = (bf16[1024,256]{1,0:T(8,128)(2,1)S(1)}, bf16[1024,256]{1,0:T(8,128)(2,1)}, u32[]{:S(2)}) copy-start(bf16[1024,256]{1,0:T(8,128)(2,1)} %param.7) | copy-start | bytes 1572868
  6.5 27.7 %slice-start = ((s8[5242880]{0:T(1024)(128)(4,1)}), s8[1048576]{0:T(1024)(128)(4,1)S(1)}, s32[]{:S(2)}) async-start(s8[5242880]{0:T(1024)(128)(4,1)} %bitcast.104), calls=%async_computation.2 | async-start | bytes 2097152
  6.5 169.4 %reduce-scatter.2.cloned.1.call-start = ((), (), s32[]{:S(2)}) async-start(), calls=%async_computation.1 | async-start | bytes 10485760 | tf_op jit(solution)/shard_map/reduce_scatter | solution.py:47
  6.5 24.7 %collective-permute-start.3 = (bf16[256,2048]{1,0:T(8,128)(2,1)}, bf16[256,2048]{1,0:T(8,128)(2,1)}, u32[]{:S(2)}, u32[]{:S(2)}) collective-permute-start(bf16[256,2048]{1,0:T(8,128)(2,1)} %bitcast.94), channel_id=1, source_target_pairs={{0,32},{4,36},{8,40},{12,44},{16,48},{20,52},{24,56},{28,60},{32,0... | collective-permute-start | bytes 3145736 | tf_op jit(solution)/shard_map/ppermute | solution.py:8
  8.6 31.4 %collective-permute-start.2 = (bf16[256,2048]{1,0:T(8,128)(2,1)}, bf16[256,2048]{1,0:T(8,128)(2,1)}, u32[]{:S(2)}, u32[]{:S(2)}) collective-permute-start(bf16[256,2048]{1,0:T(8,128)(2,1)} %bitcast.95), channel_id=1, source_target_pairs={{0,16},{4,20},{8,24},{12,28},{16,0},{20,4},{24,8},{28,12},{32,48},... | collective-permute-start | bytes 3145736 | tf_op jit(solution)/shard_map/ppermute | solution.py:8
  11.5 45.4 %collective-permute-start.1 = (bf16[256,2048]{1,0:T(8,128)(2,1)}, bf16[256,2048]{1,0:T(8,128)(2,1)}, u32[]{:S(2)}, u32[]{:S(2)}) collective-permute-start(bf16[256,2048]{1,0:T(8,128)(2,1)} %bitcast.96), channel_id=1, source_target_pairs={{0,8},{4,12},{8,0},{12,4},{16,24},{20,28},{24,16},{28,20},{32,40},... | collective-permute-start | bytes 3145736 | tf_op jit(solution)/shard_map/ppermute | solution.py:8
  11.9 53.7 %collective-permute-start = (bf16[256,2048]{1,0:T(8,128)(2,1)}, bf16[256,2048]{1,0:T(8,128)(2,1)S(1)}, u32[]{:S(2)}, u32[]{:S(2)}) collective-permute-start(bf16[256,2048]{1,0:T(8,128)(2,1)} %bitcast.97), channel_id=1, source_target_pairs={{0,4},{4,0},{8,12},{12,8},{16,20},{20,16},{24,28},{28,24},{32,36},... | collective-permute-start | bytes 3145736 | tf_op jit(solution)/shard_map/ppermute | solution.py:8
  15.5 57.6 %collective-permute-start.4 = (bf16[256,2048]{1,0:T(8,128)(2,1)}, bf16[256,2048]{1,0:T(8,128)(2,1)}, u32[]{:S(2)}, u32[]{:S(2)}) collective-permute-start(bf16[256,2048]{1,0:T(8,128)(2,1)} %bitcast.98), channel_id=1, source_target_pairs={{0,64},{4,68},{8,72},{12,76},{16,80},{20,84},{24,88},{28,92},{32,9... | collective-permute-start | bytes 3145736 | tf_op jit(solution)/shard_map/ppermute | solution.py:8
  19.9 14.4 %slice-start.1 = ((s8[5242880]{0:T(1024)(128)(4,1)}), s8[4194304]{0:T(1024)(128)(4,1)S(1)}, s32[]{:S(2)}) async-start(s8[5242880]{0:T(1024)(128)(4,1)} %bitcast.104), calls=%async_computation.3 | async-start | bytes 8388608
  76.1 103.1 %copy-start.1 = (bf16[1024,256]{1,0:T(8,128)(2,1)S(1)}, bf16[1024,256]{1,0:T(8,128)(2,1)}, u32[]{:S(2)}) copy-start(bf16[1024,256]{1,0:T(8,128)(2,1)} %param.7) | copy-start | bytes 1572868
  94.5 81.5 %copy-start.2 = (bf16[1,256,2048]{2,1,0:T(8,128)(2,1)S(1)}, bf16[1,256,2048]{2,1,0:T(8,128)(2,1)}, u32[]{:S(2)}) copy-start(bf16[1,256,2048]{2,1,0:T(8,128)(2,1)} %param.6) | copy-start | bytes 3145732
Sparse Core Ops, SparseCore 0:
  94.6 81.2 reduce-scatter.1
where the time goes:
time: 186 us
  waiting for transfers between devices  94.4 us (51%)
  matrix products  45.9 us (25%)
  local copies, waits for them, and re-layouts  15.1 us (8%)
  between operations  14.2 us (8%)
  starting transfers between devices  11.4 us (6%)
  other arithmetic  5.07 us (3%)
    reduce_scatter x1, waiting for transfers between devices, per_device(): lax.psum_scatter(jnp.dot(h_imp, local, preferred_element_type=jnp.float32...  80.7 us
    dot_general x5, matrix products, per_device(): jnp.dot(matrix, partner, preferred_element_type=jnp.float32)  40 us
    broadcast_in_dim x5, local copies, waits for them, and re-layouts, per_device(): jnp.repeat(jnp.repeat(columns, blk, axis=0), blk, axis=1)  14.7 us
    ppermute x5, waiting for transfers between devices, partner_2(): lax.ppermute(value, axis, [(i, i ^ 1 << stride) for i in range(lax.axis_s...  13.7 us
    ppermute x5, starting transfers between devices, partner_2(): lax.ppermute(value, axis, [(i, i ^ 1 << stride) for i in range(lax.axis_s...  11.4 us
    dot_general x1, matrix products, per_device(): jnp.dot(h_imp, local, preferred_element_type=jnp.float32) + total  5.88 us
  transfers between devices with their start and end apart: 6, of which 3 were waited for; matrix products, arithmetic and copies ran while one was open for 22% of the time, Pallas kernels for 0%

commit v1 on v0

v1 whole, which is shorter than its diff:
```python
import jax
import jax.numpy as jnp
from jax import lax
from jax.experimental import pallas as pl
from jax.experimental.pallas import tpu as pltpu
from jax.sharding import PartitionSpec as P

MESH = pl.DeviceIdType.MESH
CHUNKS = 4
LEAST = 1e-30
TOP = 32767.0


def flip(index, bit):
    return index + bit - 2 * bit * ((index // bit) % 2)


def kernel(
    psi, h_imp, hops, patterns, signs, energy, out,
    raw, weights, amps, kept, other, coded, scales, coded_in, scales_in, stage,
    own_sem, mat_sem, near_send, near_recv, pair_send, pair_recv, pass_send, pass_recv,
    sum_send, sum_recv, end_send, end_recv, op_send, op_recv,
):
    bath, imp = lax.axis_index("bath"), lax.axis_index("imp")
    z_lo, core = imp // 2, imp % 2
    side = [(bath // (1 << level)) % 2 for level in range(5)]
    rows, rest = psi.shape
    half = rest // 2
    width = half // CHUNKS
    chip_rows = 2 * rows
    blk = 128

    sibling = (bath, flip(imp, 1))
    across = (bath, flip(imp, 2))
    near = [
        [(flip(bath, 2), z_lo * 2 + q) for q in range(2)],
        [(flip(bath, 8), z_lo * 2 + q) for q in range(2)],
        [(flip(bath, 1), (1 - z_lo) * 2 + q) for q in range(2)],
    ]
    onward = [(flip(flip(bath, 2), 4), imp), (flip(flip(bath, 8), 16), imp)]
    near_slot = (1, 3, 5)
    onward_slot = (2, 4)

    def slot_rows(slot, q):
        return pl.ds(pl.multiple_of(slot * chip_rows + q * rows, rows), rows)

    def columns(q, j):
        return pl.ds(pl.multiple_of(q * half + j * width, 128), width)

    def remote(src, dst, send, recv, device):
        return pltpu.make_async_remote_copy(
            src_ref=src, dst_ref=dst, send_sem=send, recv_sem=recv, device_id=device, device_id_type=MESH
        )

    own = [
        pltpu.make_async_copy(psi.at[:, columns(core, j)], amps.at[j, slot_rows(0, core), :], own_sem.at[j])
        for j in range(CHUNKS)
    ]
    mats = [pltpu.make_async_copy(h_imp, weights.at[:, slot_rows(0, core)], mat_sem.at[0])]
    for level in range(1, 5):
        mats.append(pltpu.make_async_copy(hops.at[side[level], level], raw.at[level, core], mat_sem.at[level]))
    for copy in mats + own:
        copy.start()

    barrier = pltpu.get_barrier_semaphore()
    peers = [sibling, across] + near[0] + near[1] + near[2] + onward
    for peer in peers:
        pl.semaphore_signal(barrier, inc=1, device_id=peer, device_id_type=MESH)
    pl.semaphore_wait(barrier, len(peers))

    def near_copy(a, j, q):
        return remote(
            psi.at[:, columns(q, j)],
            amps.at[j, slot_rows(near_slot[a], core), :],
            near_send.at[a, j, q],
            near_recv.at[a, j, core],
            near[a][q],
        )

    def near_wait(a, j):
        for q in range(2):
            remote(
                psi.at[:, columns(q, j)],
                amps.at[j, slot_rows(near_slot[a], q), :],
                near_send.at[a, j, q],
                near_recv.at[a, j, q],
                near[a][q],
            ).wait_recv()

    def pair_copy(j):
        return remote(
            psi.at[:, columns(1 - core, j)],
            amps.at[j, slot_rows(0, core), :],
            pair_send.at[j],
            pair_recv.at[j],
            sibling,
        )

    def pair_wait(j):
        remote(
            psi.at[:, columns(core, j)],
            amps.at[j, slot_rows(0, 1 - core), :],
            pair_send.at[j],
            pair_recv.at[j],
            sibling,
        ).wait_recv()

    def pass_copy(a, j):
        src = pl.ds(near_slot[a] * chip_rows, chip_rows)
        dst = pl.ds(onward_slot[a] * chip_rows, chip_rows)
        return remote(
            amps.at[j, src, :], amps.at[j, dst, :], pass_send.at[a, j], pass_recv.at[a, j], onward[a]
        )

    def sum_copy(j):
        return (
            remote(coded.at[j], coded_in.at[j], sum_send.at[j, 0], sum_recv.at[j, 0], across),
            remote(scales.at[j], scales_in.at[j], sum_send.at[j, 1], sum_recv.at[j, 1], across),
        )

    def end_copy(j):
        return remote(stage.at[j], out.at[:, columns(core, j)], end_send.at[j], end_recv.at[j], sibling)

    def end_wait(j):
        remote(
            stage.at[j], out.at[:, columns(1 - core, j)], end_send.at[j], end_recv.at[j], sibling
        ).wait_recv()

    op0 = remote(hops.at[side[0], 0], raw.at[0, core], op_send.at[0], op_recv.at[0], across)
    op0_on = remote(raw.at[0, core], raw.at[0, core], op_send.at[6], op_recv.at[6], sibling)
    ops = [
        remote(h_imp, weights.at[:, slot_rows(0, core)], op_send.at[5], op_recv.at[5], sibling)
    ]
    for level in range(1, 5):
        ops.append(
            remote(
                hops.at[side[level], level], raw.at[level, core], op_send.at[level], op_recv.at[level], sibling
            )
        )

    for j in range(CHUNKS):
        for q in range(2):
            for a in range(3):
                near_copy(a, j, q).start()
        if j == 0:
            op0.start()
            pair_copy(0).start()
            for copy in ops:
                copy.start()
        else:
            pair_copy(j).start()

    def mask(level, slot, q, from_z):
        def block(p, carry):
            sign = (1 - 2 * signs[level, 0, p]).astype(jnp.float32)
            for k in range(rows // blk):
                keep = patterns[side[level], level, p, from_z * 4 + q * 2 + k].astype(jnp.float32)
                factor = jnp.full((blk, blk), keep * sign, jnp.float32).astype(jnp.bfloat16)
                at = pl.ds(pl.multiple_of(p * blk, blk), blk)
                to = pl.ds(pl.multiple_of(slot * chip_rows + q * rows + k * blk, blk), blk)
                weights[at, to] = raw[level, q, at, k * blk : (k + 1) * blk] * factor
            return carry

        lax.fori_loop(0, 8, block, 0)

    for level in range(1, 5):
        mats[level].wait()
        mask(level, level, core, z_lo)
    for level in range(1, 5):
        ops[level].wait_recv()
        mask(level, level, 1 - core, z_lo)
    mats[0].wait()
    ops[0].wait_recv()
    op0.wait_recv()
    op0_on.start()
    mask(0, 5, core, 1 - z_lo)

    def forward(j):
        for a in range(2):
            near_wait(a, j)
            pass_copy(a, j).start()

    def product(z, j):
        at = pl.ds(pl.multiple_of(z * chip_rows, chip_rows), chip_rows)
        return jnp.dot(weights[at, :], amps[j], preferred_element_type=jnp.float32)

    def compute(j):
        own[j].wait()
        pair_wait(j)
        near_wait(2, j)
        for a in range(2):
            pass_copy(a, j).wait_recv()
        other[...] = product(1 - z_lo, j)
        value = other[...]
        most = jnp.maximum(jnp.max(jnp.abs(value), axis=0, keepdims=True), LEAST)
        scales[j] = jnp.broadcast_to(most * (1.0 / TOP), (8, width))
        coded[j] = jnp.round(value * (TOP / most)).astype(jnp.int32).astype(jnp.int16)
        for copy in sum_copy(j):
            copy.start()
        kept[j] = product(z_lo, j)

    def finish(j):
        for copy in sum_copy(j):
            copy.wait_recv()
        scale = scales_in[j, 0:1, :]
        e = energy[0]

        def total(q):
            at = pl.ds(pl.multiple_of(q * rows, rows), rows)
            return (
                kept[j, at, :]
                + coded_in[j, at, :].astype(jnp.int32).astype(jnp.float32) * scale
                + e * amps[j, at, :].astype(jnp.float32)
            )

        stage[j] = total(1 - core)
        end_copy(j).start()
        out[:, columns(core, j)] = total(core)

    forward(0)
    for j in range(CHUNKS):
        if j + 1 < CHUNKS:
            forward(j + 1)
        if j == 0:
            op0_on_in = remote(
                raw.at[0, core], raw.at[0, 1 - core], op_send.at[6], op_recv.at[6], sibling
            )
            op0_on_in.wait_recv()
            mask(0, 5, 1 - core, 1 - z_lo)
        compute(j)
        if j >= 1:
            finish(j - 1)
    finish(CHUNKS - 1)

    for copy in ops + [op0, op0_on]:
        copy.wait_send()
    for j in range(CHUNKS):
        for a in range(3):
            for q in range(2):
                near_copy(a, j, q).wait_send()
        for a in range(2):
            pass_copy(a, j).wait_send()
        pair_copy(j).wait_send()
        for copy in sum_copy(j):
            copy.wait_send()
        end_copy(j).wait_send()
        end_wait(j)


def per_device(psi, h_imp, hops, patterns, signs, bath_energy):
    local = psi[0]
    rows, rest = local.shape
    imps = h_imp.shape[0]
    half = rest // 2
    width = half // CHUNKS
    dma = pltpu.SemaphoreType.DMA
    anywhere = pl.BlockSpec(memory_space=pl.ANY)
    scalar = pl.BlockSpec(memory_space=pltpu.SMEM)
    applied = pl.pallas_call(
        kernel,
        out_shape=jax.ShapeDtypeStruct((rows, rest), jnp.float32),
        in_specs=[anywhere, anywhere, anywhere, scalar, scalar, scalar],
        out_specs=pl.BlockSpec(memory_space=pltpu.VMEM),
        scratch_shapes=[
            pltpu.VMEM((5, 2, imps, rows), jnp.bfloat16),
            pltpu.VMEM((imps, 12 * rows), jnp.bfloat16),
            pltpu.VMEM((CHUNKS, 12 * rows, width), jnp.bfloat16),
            pltpu.VMEM((CHUNKS, 2 * rows, width), jnp.float32),
            pltpu.VMEM((2 * rows, width), jnp.float32),
            pltpu.VMEM((CHUNKS, 2 * rows, width), jnp.int16),
            pltpu.VMEM((CHUNKS, 8, width), jnp.float32),
            pltpu.VMEM((CHUNKS, 2 * rows, width), jnp.int16),
            pltpu.VMEM((CHUNKS, 8, width), jnp.float32),
            pltpu.VMEM((CHUNKS, rows, width), jnp.float32),
            dma((CHUNKS,)),
            dma((5,)),
            dma((3, CHUNKS, 2)),
            dma((3, CHUNKS, 2)),
            dma((CHUNKS,)),
            dma((CHUNKS,)),
            dma((2, CHUNKS)),
            dma((2, CHUNKS)),
            dma((CHUNKS, 2)),
            dma((CHUNKS, 2)),
            dma((CHUNKS,)),
            dma((CHUNKS,)),
            dma((7,)),
            dma((7,)),
        ],
        compiler_params=pltpu.CompilerParams(
            collective_id=0, has_side_effects=True, vmem_limit_bytes=50 * 1024 * 1024
        ),
    )(local, h_imp, hops, patterns, signs, bath_energy)
    return applied[None]


def solution(mesh):
    placed = (
        P("bath", "imp", None),
        P(None, "imp"),
        P(None, None, None, "imp"),
        P(),
        P(None, "bath", None),
        P("bath"),
    )
    return jax.shard_map(
        per_device, mesh=mesh, in_specs=placed, out_specs=P("bath", "imp", None), check_vma=False
    )
```

time: 186 us -> 63.9 us (0.34)
  waiting for transfers between devices: 94.4 us -> 0 us
  Pallas kernels: 0 us -> 57.9 us
  matrix products: 45.9 us -> 0 us
  between operations: 14.2 us -> 0.67 us
  starting transfers between devices: 11.4 us -> 0 us
  local copies, waits for them, and re-layouts: 15.1 us -> 5.04 us
  other arithmetic: 5.07 us -> 0 us
    reduce_scatter x1 -> x0, waiting for transfers between devices: 80.7 us -> none  [per_device(): lax.psum_scatter(jnp.dot(h_imp, local, preferred_element_type=jnp.float32...]
    pallas_call x0 -> x1, Pallas kernels: none -> 57.9 us  [per_device(): pl.pallas_call(kernel, out_shape=jax.ShapeDtypeStruct((rows, rest), jnp.f...]
    dot_general x6 -> x0, matrix products: 45.9 us -> none  [the longest x5 40 us: per_device(): jnp.dot(matrix, partner, preferred_element_type=jnp.float32)]
    broadcast_in_dim x10 -> x0, local copies, waits for them, and re-layouts: 14.9 us -> none  [the longest x5 14.7 us: per_device(): jnp.repeat(jnp.repeat(columns, blk, axis=0), blk, axis=1)]
    ppermute x5 -> x0, waiting for transfers between devices: 13.7 us -> none  [partner_2(): lax.ppermute(value, axis, [(i, i ^ 1 << stride) for i in range(lax.axis_s...]
    ppermute x5 -> x0, starting transfers between devices: 11.4 us -> none  [partner_2(): lax.ppermute(value, axis, [(i, i ^ 1 << stride) for i in range(lax.axis_s...]
    unnamed x10 -> x9, local copies, waits for them, and re-layouts: 0.02 us -> 5.04 us
    broadcast_in_dim x1 -> x0, other arithmetic: 3.29 us -> none  [per_device(): return applied[None]]
  transfers between devices with their start and end apart: 6 -> 0, of which waited for: 3 -> 0; matrix products, arithmetic and copies ran while one was open for 22% -> 0% of each run, Pallas kernels for 0% -> 0%
where the time goes in v1:
time: 63.9 us; the launch traced here: 63.6 us
  Pallas kernels  57.9 us (91%)
  local copies, waits for them, and re-layouts  5.04 us (8%)
  between operations  0.67 us (1%)
    pallas_call x1, Pallas kernels, per_device(): pl.pallas_call(kernel, out_shape=jax.ShapeDtypeStruct((rows, rest), jnp.f...  57.9 us
    unnamed x9, local copies, waits for them, and re-layouts  5.04 us

profile of v1, /device:TPU:1, one launch (start us, length us, event | category | flops | bytes accessed | tf_op | source)
XLA Modules:
  0.0 63.6 jit_solution(12956249298214034247)
XLA Ops:
  0.7 0.0 copy-start
  0.7 1.2 %copy-done = bf16[1,256,2048]{2,1,0:T(8,128)(2,1)S(1)} copy-done((bf16[1,256,2048]{2,1,0:T(8,128)(2,1)S(1)}, bf16[1,256,2048]{2,1,0:T(8,128)(2,1)}, u32[]{:S(2)}) %copy-start) | copy-done | bytes 1048600
  1.9 0.0 copy-start.1
  1.9 1.0 %copy-done.1 = bf16[1024,256]{1,0:T(8,128)(2,1)S(1)} copy-done((bf16[1024,256]{1,0:T(8,128)(2,1)S(1)}, bf16[1024,256]{1,0:T(8,128)(2,1)}, u32[]{:S(2)}) %copy-start.1) | copy-done | bytes 524312
  2.9 0.0 copy-start.2
  2.9 0.8 %copy-done.2 = s32[2,5,8,8]{3,2,1,0:T(8,128)S(1)} copy-done((s32[2,5,8,8]{3,2,1,0:T(8,128)S(1)}, s32[2,5,8,8]{3,2,1,0:T(8,128)}, u32[]{:S(2)}) %copy-start.2) | copy-done | bytes 2584
  3.7 0.0 copy-start.3
  3.7 0.7 %copy-done.3 = s32[5,1,8]{2,1,0:T(1,128)S(1)} copy-done((s32[5,1,8]{2,1,0:T(1,128)S(1)}, s32[5,1,8]{2,1,0:T(1,128)}, u32[]{:S(2)}) %copy-start.3) | copy-done | bytes 184
  4.4 57.9 %shard_map.64 = f32[256,2048]{1,0:T(8,128)S(1)} custom-call(bf16[256,2048]{1,0:T(8,128)(2,1)S(1)} %bitcast.3, bf16[1024,256]{1,0:T(8,128)(2,1)S(1)} %copy-done.1, bf16[2,5,1024,256]{3,2,1,0:T(8,128)(2,1)} %hops.1, s32[2,5,8,8]{3,2,1,0:T(8,128)S(1)} %copy-done.2, s32[5,1,8]{2,1,0:T(1,128)S(1)} %copy-done.3, f32[1]{0:T(128)S(6)} %copy.8.energy), custom_call_target="tpu_custom_call" | custom-call | tf_op jit(solution)/shard_map/pallas_call | solution.py:259
  62.3 1.3 %copy.9 = f32[1,256,2048]{2,1,0:T(8,128)} copy(f32[1,256,2048]{2,1,0:T(8,128)S(1)} %bitcast.2) | data formatting | bytes 4194304
Async XLA Ops:
  0.7 1.2 %copy-start = (bf16[1,256,2048]{2,1,0:T(8,128)(2,1)S(1)}, bf16[1,256,2048]{2,1,0:T(8,128)(2,1)}, u32[]{:S(2)}) copy-start(bf16[1,256,2048]{2,1,0:T(8,128)(2,1)} %param.6) | copy-start | bytes 3145732
  1.9 1.0 %copy-start.1 = (bf16[1024,256]{1,0:T(8,128)(2,1)S(1)}, bf16[1024,256]{1,0:T(8,128)(2,1)}, u32[]{:S(2)}) copy-start(bf16[1024,256]{1,0:T(8,128)(2,1)} %h_imp.1) | copy-start | bytes 1572868
  2.9 0.8 %copy-start.2 = (s32[2,5,8,8]{3,2,1,0:T(8,128)S(1)}, s32[2,5,8,8]{3,2,1,0:T(8,128)}, u32[]{:S(2)}) copy-start(s32[2,5,8,8]{3,2,1,0:T(8,128)} %patterns.1) | copy-start | bytes 7684
  3.7 0.7 %copy-start.3 = (s32[5,1,8]{2,1,0:T(1,128)S(1)}, s32[5,1,8]{2,1,0:T(1,128)}, u32[]{:S(2)}) copy-start(s32[5,1,8]{2,1,0:T(1,128)} %signs.1) | copy-start | bytes 484

commit v2 on v1

v2 whole, which is shorter than its diff:
```python
import jax
import jax.numpy as jnp
from jax import lax
from jax.experimental import pallas as pl
from jax.experimental.pallas import tpu as pltpu
from jax.sharding import PartitionSpec as P

MESH = pl.DeviceIdType.MESH
CHUNKS = 8
LEAST = 1e-30
TOP = 32767.0
AHEAD = 2
BEHIND = 2
BLK = 128


def flip(index, bit):
    return index + bit - 2 * bit * ((index // bit) % 2)


def kernel(
    psi, h_imp, hops, patterns_in, signs_in, energy, out,
    raw, weights, amps, local, kept, stage, coded, scales, coded_in, scales_in, patterns, signs,
    own_sem, mat_sem, small_sem, near_send, near_recv, pair_send, pair_recv, pass_send, pass_recv,
    sum_send, sum_recv, kept_send, kept_recv, op_send, op_recv, zero_send, zero_recv,
):
    bath, imp = lax.axis_index("bath"), lax.axis_index("imp")
    z_lo, core = imp // 2, imp % 2
    side = [(bath // (1 << level)) % 2 for level in range(5)]
    rows, rest = psi.shape
    half = rest // 2
    width = half // CHUNKS
    chip_rows = 2 * rows

    sibling = (bath, flip(imp, 1))
    across = [(bath, (1 - z_lo) * 2 + q) for q in range(2)]
    near = [
        [(flip(bath, 2), z_lo * 2 + q) for q in range(2)],
        [(flip(bath, 8), z_lo * 2 + q) for q in range(2)],
        [(flip(bath, 1), (1 - z_lo) * 2 + q) for q in range(2)],
    ]
    across_same = (bath, flip(imp, 2))
    near_same = (flip(bath, 1), flip(imp, 2))
    onward = [(flip(flip(bath, 2), 4), imp), (flip(flip(bath, 8), 16), imp)]
    near_slot = (1, 3, 5)
    onward_slot = (2, 4)

    def slot_rows(slot, q):
        return pl.ds(pl.multiple_of(slot * chip_rows + q * rows, rows), rows)

    def columns(q, j):
        return pl.ds(pl.multiple_of(q * half + j * width, 128), width)

    def chip(z):
        return pl.ds(pl.multiple_of(z * chip_rows, chip_rows), chip_rows)

    def remote(src, dst, send, recv, device):
        return pltpu.make_async_remote_copy(
            src_ref=src, dst_ref=dst, send_sem=send, recv_sem=recv, device_id=device, device_id_type=MESH
        )

    small = [
        pltpu.make_async_copy(patterns_in, patterns, small_sem.at[0]),
        pltpu.make_async_copy(signs_in, signs, small_sem.at[1]),
    ]
    own = [
        pltpu.make_async_copy(psi.at[:, columns(core, j)], amps.at[j, slot_rows(0, core), :], own_sem.at[j])
        for j in range(CHUNKS)
    ]
    whole = pltpu.make_async_copy(psi, local, small_sem.at[2])
    mats = [pltpu.make_async_copy(h_imp, weights.at[:, slot_rows(0, core)], mat_sem.at[0])]
    for level in range(1, 5):
        mats.append(pltpu.make_async_copy(hops.at[side[level], level], raw.at[level, core], mat_sem.at[level]))
    for copy in small + mats + own + [whole]:
        copy.start()

    barrier = pltpu.get_barrier_semaphore()
    peers = [sibling] + across + near[0] + near[1] + near[2] + onward
    for peer in peers:
        pl.semaphore_signal(barrier, inc=1, device_id=peer, device_id_type=MESH)
    pl.semaphore_wait(barrier, len(peers))

    def near_copy(a, j, q, source):
        return remote(
            psi.at[:, columns(q, j)],
            amps.at[j, slot_rows(near_slot[a], source), :],
            near_send.at[a, j, q],
            near_recv.at[a, j, source],
            near[a][q],
        )

    def near_wait(a, j):
        for q in range(2):
            near_copy(a, j, q, q).wait_recv()

    def pair_copy(j, source):
        return remote(
            psi.at[:, columns(1 - core, j)],
            amps.at[j, slot_rows(0, source), :],
            pair_send.at[j],
            pair_recv.at[j],
            sibling,
        )

    def pass_copy(a, j):
        src = pl.ds(near_slot[a] * chip_rows, chip_rows)
        dst = pl.ds(onward_slot[a] * chip_rows, chip_rows)
        return remote(
            amps.at[j, src, :], amps.at[j, dst, :], pass_send.at[a, j], pass_recv.at[a, j], onward[a]
        )

    def sum_copy(j, q, source):
        return (
            remote(
                coded.at[j, q], coded_in.at[j, source], sum_send.at[j, q, 0], sum_recv.at[j, source, 0], across[q]
            ),
            remote(
                scales.at[j, q], scales_in.at[j, source], sum_send.at[j, q, 1], sum_recv.at[j, source, 1], across[q]
            ),
        )

    def kept_copy(j, source):
        return remote(stage.at[j], kept.at[j, source], kept_send.at[j], kept_recv.at[j], sibling)

    zero = [
        remote(
            hops.at[side[0], 0, chip(z_lo), :], raw.at[0, core, chip(z_lo), :],
            zero_send.at[0], zero_recv.at[0], across_same,
        ),
        remote(
            hops.at[1 - side[0], 0, chip(1 - z_lo), :], raw.at[0, core, chip(1 - z_lo), :],
            zero_send.at[1], zero_recv.at[1], near_same,
        ),
    ]
    zero_in = [
        remote(
            hops.at[side[0], 0, chip(1 - z_lo), :], raw.at[0, core, chip(1 - z_lo), :],
            zero_send.at[0], zero_recv.at[0], across_same,
        ),
        remote(
            hops.at[side[0], 0, chip(z_lo), :], raw.at[0, core, chip(z_lo), :],
            zero_send.at[1], zero_recv.at[1], near_same,
        ),
    ]

    def zero_on(i, source):
        at = chip(1 - z_lo) if i == 0 else chip(z_lo)
        return remote(
            raw.at[0, core, at, :], raw.at[0, source, at, :], zero_send.at[2 + i], zero_recv.at[2 + i], sibling
        )

    ops = [remote(h_imp, weights.at[:, slot_rows(0, core)], op_send.at[0], op_recv.at[0], sibling)]
    for level in range(1, 5):
        ops.append(
            remote(
                hops.at[side[level], level], raw.at[level, core], op_send.at[level], op_recv.at[level], sibling
            )
        )

    zero[0].start()
    zero[1].start()
    for j in range(CHUNKS):
        for q in range(2):
            for a in range(3):
                near_copy(a, j, q, core).start()
        pair_copy(j, core).start()
        if j == 0:
            for copy in ops:
                copy.start()

    def mask(level, slot, q, from_z, first, count):
        def block(p, carry):
            sign = (1 - 2 * signs[level, 0, first + p]).astype(jnp.float32)
            at = pl.ds(pl.multiple_of((first + p) * BLK, BLK), BLK)
            for k in range(rows // BLK):
                keep = patterns[side[level], level, first + p, from_z * 4 + q * 2 + k].astype(jnp.float32)
                factor = jnp.full((BLK, BLK), keep * sign, jnp.float32).astype(jnp.bfloat16)
                to = pl.ds(pl.multiple_of(slot * chip_rows + q * rows + k * BLK, BLK), BLK)
                weights[at, to] = raw[level, q, at, k * BLK : (k + 1) * BLK] * factor
            return carry

        lax.fori_loop(0, count, block, 0)

    def forward(j):
        for a in range(2):
            near_wait(a, j)
            pass_copy(a, j).start()

    def product(z, q, j):
        at = pl.ds(pl.multiple_of(z * chip_rows + q * rows, rows), rows)
        return jnp.dot(weights[at, :], amps[j], preferred_element_type=jnp.float32)

    def compute(j):
        own[j].wait()
        pair_copy(j, core).wait_recv()
        near_wait(2, j)
        for a in range(2):
            pass_copy(a, j).wait_recv()
        for q in range(2):
            value = product(1 - z_lo, q, j)
            most = jnp.maximum(jnp.max(jnp.abs(value), axis=0, keepdims=True), LEAST)
            scales[j, q] = most * (1.0 / TOP)
            coded[j, q] = jnp.round(value * (TOP / most)).astype(jnp.int32).astype(jnp.int16)
            for copy in sum_copy(j, q, core):
                copy.start()
        stage[j] = product(z_lo, 1 - core, j)
        kept_copy(j, core).start()
        kept[j, core] = product(z_lo, core, j)

    def finish(j):
        kept_copy(j, core).wait_recv()
        e = energy[0]
        for q in range(2):
            for copy in sum_copy(j, q, q):
                copy.wait_recv()
            at = slice(q * half + j * width, q * half + (j + 1) * width)
            out[:, at] = (
                kept[j, q]
                + coded_in[j, q].astype(jnp.int32).astype(jnp.float32) * scales_in[j, q]
                + e * local[:, at].astype(jnp.float32)
            )

    for copy in small:
        copy.wait()
    for level in range(1, 5):
        mats[level].wait()
        mask(level, level, core, z_lo, 0, 8)
    forward(0)
    for level in range(1, 5):
        ops[level].wait_recv()
        mask(level, level, 1 - core, z_lo, 0, 8)
    mats[0].wait()
    ops[0].wait_recv()
    whole.wait()
    for j in range(1, AHEAD):
        forward(j)
    for i in range(2):
        zero_in[i].wait_recv()
        zero_on(i, core).start()
        mask(0, 5, core, 1 - z_lo, ((1 - z_lo) if i == 0 else z_lo) * 4, 4)
    for i in range(2):
        zero_on(i, 1 - core).wait_recv()
        mask(0, 5, 1 - core, 1 - z_lo, ((1 - z_lo) if i == 0 else z_lo) * 4, 4)

    for j in range(CHUNKS):
        if j + AHEAD < CHUNKS:
            forward(j + AHEAD)
        compute(j)
        if j >= BEHIND:
            finish(j - BEHIND)
    for j in range(CHUNKS - BEHIND, CHUNKS):
        finish(j)

    for copy in ops + zero + [zero_on(i, core) for i in range(2)]:
        copy.wait_send()
    for j in range(CHUNKS):
        for q in range(2):
            for a in range(3):
                near_copy(a, j, q, core).wait_send()
            for copy in sum_copy(j, q, core):
                copy.wait_send()
        for a in range(2):
            pass_copy(a, j).wait_send()
        pair_copy(j, core).wait_send()
        kept_copy(j, core).wait_send()


def per_device(psi, h_imp, hops, patterns, signs, bath_energy):
    here = psi[0]
    rows, rest = here.shape
    imps = h_imp.shape[0]
    width = rest // 2 // CHUNKS
    n = CHUNKS
    dma = pltpu.SemaphoreType.DMA
    anywhere = pl.BlockSpec(memory_space=pltpu.HBM)
    scalar = pl.BlockSpec(memory_space=pltpu.SMEM)
    operands = [pltpu.with_memory_space_constraint(x, pltpu.HBM) for x in (here, h_imp, hops, patterns, signs)]
    applied = pl.pallas_call(
        kernel,
        out_shape=pltpu.VMEM((rows, rest), jnp.float32),
        in_specs=[anywhere] * 5 + [scalar],
        out_specs=pl.BlockSpec(memory_space=pltpu.VMEM),
        scratch_shapes=[
            pltpu.VMEM((5, 2, imps, rows), jnp.bfloat16),
            pltpu.VMEM((imps, 12 * rows), jnp.bfloat16),
            pltpu.VMEM((n, 12 * rows, width), jnp.bfloat16),
            pltpu.VMEM((rows, rest), jnp.bfloat16),
            pltpu.VMEM((n, 2, rows, width), jnp.float32),
            pltpu.VMEM((n, rows, width), jnp.float32),
            pltpu.VMEM((n, 2, rows, width), jnp.int16),
            pltpu.VMEM((n, 2, 1, width), jnp.float32),
            pltpu.VMEM((n, 2, rows, width), jnp.int16),
            pltpu.VMEM((n, 2, 1, width), jnp.float32),
            pltpu.SMEM(patterns.shape, jnp.int32),
            pltpu.SMEM(signs.shape, jnp.int32),
            dma((n,)), dma((5,)), dma((3,)),
            dma((3, n, 2)), dma((3, n, 2)),
            dma((n,)), dma((n,)),
            dma((2, n)), dma((2, n)),
            dma((n, 2, 2)), dma((n, 2, 2)),
            dma((n,)), dma((n,)),
            dma((5,)), dma((5,)),
            dma((4,)), dma((4,)),
        ],
        compiler_params=pltpu.CompilerParams(
            collective_id=0, has_side_effects=True, vmem_limit_bytes=50 * 1024 * 1024
        ),
    )(*operands, bath_energy)
    return applied[None]


def solution(mesh):
    placed = (
        P("bath", "imp", None),
        P(None, "imp"),
        P(None, None, None, "imp"),
        P(),
        P(None, "bath", None),
        P("bath"),
    )
    return jax.shard_map(
        per_device, mesh=mesh, in_specs=placed, out_specs=P("bath", "imp", None), check_vma=False
    )
```

time: 63.9 us -> 46.3 us (0.72)
  Pallas kernels: 57.9 us -> 44.2 us
  local copies, waits for them, and re-layouts: 5.04 us -> 1.32 us
    pallas_call x1, Pallas kernels: 57.9 us -> 44.2 us  [per_device(): pl.pallas_call(kernel, out_shape=pltpu.VMEM((rows, rest), jnp.float32), i...]
    unnamed x9 -> x1, local copies, waits for them, and re-layouts: 5.04 us -> 1.32 us
where the time goes in v2:
time: 46.3 us; the launch traced here: 46.2 us
  Pallas kernels  44.2 us (95%)
  local copies, waits for them, and re-layouts  1.32 us (3%)
  between operations  0.66 us (1%)
    pallas_call x1, Pallas kernels, per_device(): pl.pallas_call(kernel, out_shape=pltpu.VMEM((rows, rest), jnp.float32), i...  44.2 us
    unnamed x1, local copies, waits for them, and re-layouts  1.32 us

profile of v2, /device:TPU:1, one launch (start us, length us, event | category | flops | bytes accessed | tf_op | source)
XLA Modules:
  0.0 46.2 jit_solution(8840177317436842221)
XLA Ops:
  0.7 44.2 %shard_map.64 = f32[256,2048]{1,0:T(8,128)S(1)} custom-call(bf16[256,2048]{1,0:T(8,128)(2,1)} %bitcast.3, bf16[1024,256]{1,0:T(8,128)(2,1)} %h_imp.1, bf16[2,5,1024,256]{3,2,1,0:T(8,128)(2,1)} %hops.1, s32[2,5,8,8]{3,2,1,0:T(8,128)} %patterns_in.1, s32[5,1,8]{2,1,0:T(1,128)} %signs_in.1, f32[1]{0:T(128)S(6)} %copy.9.energy), custom_call_target="tpu_custom_call" | custom-call | tf_op jit(solution)/shard_map/pallas_call | solution.py:278
  44.9 1.3 %copy.8 = f32[1,256,2048]{2,1,0:T(8,128)} copy(f32[1,256,2048]{2,1,0:T(8,128)S(1)} %bitcast.2) | data formatting | bytes 4194304

commit v3 on v2

--- a/solution.py
+++ b/solution.py
@@ -10,7 +10,9 @@
 LEAST = 1e-30
 TOP = 32767.0
 AHEAD = 2
-BEHIND = 2
+BEHIND = 3
+LATE = 3
+LEFT = 128
 BLK = 128
 
 
@@ -20,9 +22,9 @@
 
 def kernel(
     psi, h_imp, hops, patterns_in, signs_in, energy, out,
-    raw, weights, amps, local, kept, stage, coded, scales, coded_in, scales_in, patterns, signs,
+    raw, weights, amps, local, kept, stage, coded, scales, coded_in, scales_in, early, patterns, signs,
     own_sem, mat_sem, small_sem, near_send, near_recv, pair_send, pair_recv, pass_send, pass_recv,
-    sum_send, sum_recv, kept_send, kept_recv, op_send, op_recv, zero_send, zero_recv,
+    sum_send, sum_recv, kept_send, kept_recv, op_send, op_recv, zero_send, zero_recv, early_send, early_recv,
 ):
     bath, imp = lax.axis_index("bath"), lax.axis_index("imp")
     z_lo, core = imp // 2, imp % 2
@@ -42,6 +44,8 @@
     across_same = (bath, flip(imp, 2))
     near_same = (flip(bath, 1), flip(imp, 2))
     onward = [(flip(flip(bath, 2), 4), imp), (flip(flip(bath, 8), 16), imp)]
+    onward_both = [[(to[0], z_lo * 2 + q) for q in range(2)] for to in onward]
+    near_as_onward = [(flip(bath, 2), imp), (flip(bath, 8), imp)]
     near_slot = (1, 3, 5)
     onward_slot = (2, 4)
 
@@ -63,19 +67,23 @@
         pltpu.make_async_copy(patterns_in, patterns, small_sem.at[0]),
         pltpu.make_async_copy(signs_in, signs, small_sem.at[1]),
     ]
-    own = [
-        pltpu.make_async_copy(psi.at[:, columns(core, j)], amps.at[j, slot_rows(0, core), :], own_sem.at[j])
-        for j in range(CHUNKS)
-    ]
+
+    def own_copy(j):
+        return pltpu.make_async_copy(psi.at[:, columns(core, j)], amps.at[j, slot_rows(0, core), :], own_sem.at[j])
+
     whole = pltpu.make_async_copy(psi, local, small_sem.at[2])
     mats = [pltpu.make_async_copy(h_imp, weights.at[:, slot_rows(0, core)], mat_sem.at[0])]
     for level in range(1, 5):
         mats.append(pltpu.make_async_copy(hops.at[side[level], level], raw.at[level, core], mat_sem.at[level]))
-    for copy in small + mats + own + [whole]:
+    for copy in small + mats + [whole]:
         copy.start()
 
+    @pl.loop(0, CHUNKS)
+    def _(j):
+        own_copy(j).start()
+
     barrier = pltpu.get_barrier_semaphore()
-    peers = [sibling] + across + near[0] + near[1] + near[2] + onward
+    peers = [sibling] + across + near[0] + near[1] + near[2] + onward_both[0] + onward_both[1]
     for peer in peers:
         pl.semaphore_signal(barrier, inc=1, device_id=peer, device_id_type=MESH)
     pl.semaphore_wait(barrier, len(peers))
@@ -122,32 +130,66 @@
     def kept_copy(j, source):
         return remote(stage.at[j], kept.at[j, source], kept_send.at[j], kept_recv.at[j], sibling)
 
-    zero = [
-        remote(
-            hops.at[side[0], 0, chip(z_lo), :], raw.at[0, core, chip(z_lo), :],
-            zero_send.at[0], zero_recv.at[0], across_same,
-        ),
-        remote(
-            hops.at[1 - side[0], 0, chip(1 - z_lo), :], raw.at[0, core, chip(1 - z_lo), :],
-            zero_send.at[1], zero_recv.at[1], near_same,
-        ),
-    ]
-    zero_in = [
-        remote(
-            hops.at[side[0], 0, chip(1 - z_lo), :], raw.at[0, core, chip(1 - z_lo), :],
-            zero_send.at[0], zero_recv.at[0], across_same,
-        ),
-        remote(
-            hops.at[side[0], 0, chip(z_lo), :], raw.at[0, core, chip(z_lo), :],
-            zero_send.at[1], zero_recv.at[1], near_same,
-        ),
-    ]
+    def early_copy(a, q, source):
+        return remote(
+            psi.at[:, columns(q, CHUNKS - 1)],
+            early.at[a, pl.ds(pl.multiple_of(source * rows, rows), rows), :],
+            early_send.at[a, q],
+            early_recv.at[a, source],
+            onward_both[a][q],
+        )
+
+    def early_pass(a):
+        dst = pl.ds(onward_slot[a] * chip_rows, chip_rows)
+        return remote(
+            early.at[a],
+            amps.at[CHUNKS - 1, dst, :],
+            pass_send.at[a, CHUNKS - 1],
+            pass_recv.at[a, CHUNKS - 1],
+            near_as_onward[a],
+        )
+
+    pieces = ((1, 0, chip_rows), (0, 0, LEFT), (0, LEFT, chip_rows - LEFT))
+
+    def piece(i, z):
+        swap, first, count = pieces[i]
+        owner = 1 - z if swap else z
+        return owner * chip_rows + first, count
+
+    def zero_copy(i):
+        first, count = piece(i, 1 - z_lo)
+        at = pl.ds(pl.multiple_of(first, BLK), count)
+        far = i == 2
+        return remote(
+            hops.at[(1 - side[0]) if far else side[0], 0, at, :], raw.at[0, core, at, :],
+            zero_send.at[i], zero_recv.at[i], near_same if far else across_same,
+        )
+
+    def zero_in(i):
+        first, count = piece(i, z_lo)
+        at = pl.ds(pl.multiple_of(first, BLK), count)
+        return remote(
+            hops.at[side[0], 0, at, :], raw.at[0, core, at, :],
+            zero_send.at[i], zero_recv.at[i], near_same if i == 2 else across_same,
+        )
 
     def zero_on(i, source):
-        at = chip(1 - z_lo) if i == 0 else chip(z_lo)
-        return remote(
-            raw.at[0, core, at, :], raw.at[0, source, at, :], zero_send.at[2 + i], zero_recv.at[2 + i], sibling
-        )
+        first, count = piece(i, z_lo)
+        at = pl.ds(pl.multiple_of(first, BLK), count)
+        return remote(
+            raw.at[0, source, at, :], raw.at[0, source, at, :], zero_send.at[3 + i], zero_recv.at[3 + i], sibling
+        )
+
+    def zero_take(i):
+        zero_in(i).wait_recv()
+        zero_on(i, core).start()
+        first, count = piece(i, z_lo)
+        mask(0, 5, core, 1 - z_lo, first // BLK, count // BLK)
+
+    def zero_rest(i):
+        zero_on(i, 1 - core).wait_recv()
+        first, count = piece(i, z_lo)
+        mask(0, 5, 1 - core, 1 - z_lo, first // BLK, count // BLK)
 
     ops = [remote(h_imp, weights.at[:, slot_rows(0, core)], op_send.at[0], op_recv.at[0], sibling)]
     for level in range(1, 5):
@@ -157,16 +199,23 @@
             )
         )
 
-    zero[0].start()
-    zero[1].start()
-    for j in range(CHUNKS):
+    zero_copy(0).start()
+    zero_copy(1).start()
+
+    def send(j):
         for q in range(2):
             for a in range(3):
                 near_copy(a, j, q, core).start()
         pair_copy(j, core).start()
-        if j == 0:
-            for copy in ops:
-                copy.start()
+
+    send(0)
+    zero_copy(2).start()
+    for a in range(2):
+        for q in range(2):
+            early_copy(a, q, core).start()
+    for copy in ops:
+        copy.start()
+    pl.loop(1, CHUNKS)(send)
 
     def mask(level, slot, q, from_z, first, count):
         def block(p, carry):
@@ -191,9 +240,15 @@
         return jnp.dot(weights[at, :], amps[j], preferred_element_type=jnp.float32)
 
     def compute(j):
-        own[j].wait()
+        own_copy(j).wait()
         pair_copy(j, core).wait_recv()
         near_wait(2, j)
+
+        @pl.when(j == CHUNKS - 1)
+        def _():
+            for a in range(2):
+                near_wait(a, j)
+
         for a in range(2):
             pass_copy(a, j).wait_recv()
         for q in range(2):
@@ -203,6 +258,8 @@
             coded[j, q] = jnp.round(value * (TOP / most)).astype(jnp.int32).astype(jnp.int16)
             for copy in sum_copy(j, q, core):
                 copy.start()
+
+    def compute_own(j):
         stage[j] = product(z_lo, 1 - core, j)
         kept_copy(j, core).start()
         kept[j, core] = product(z_lo, core, j)
@@ -213,7 +270,7 @@
         for q in range(2):
             for copy in sum_copy(j, q, q):
                 copy.wait_recv()
-            at = slice(q * half + j * width, q * half + (j + 1) * width)
+            at = columns(q, j)
             out[:, at] = (
                 kept[j, q]
                 + coded_in[j, q].astype(jnp.int32).astype(jnp.float32) * scales_in[j, q]
@@ -234,26 +291,53 @@
     whole.wait()
     for j in range(1, AHEAD):
         forward(j)
-    for i in range(2):
-        zero_in[i].wait_recv()
-        zero_on(i, core).start()
-        mask(0, 5, core, 1 - z_lo, ((1 - z_lo) if i == 0 else z_lo) * 4, 4)
-    for i in range(2):
-        zero_on(i, 1 - core).wait_recv()
-        mask(0, 5, 1 - core, 1 - z_lo, ((1 - z_lo) if i == 0 else z_lo) * 4, 4)
-
-    for j in range(CHUNKS):
-        if j + AHEAD < CHUNKS:
-            forward(j + AHEAD)
-        compute(j)
-        if j >= BEHIND:
-            finish(j - BEHIND)
-    for j in range(CHUNKS - BEHIND, CHUNKS):
-        finish(j)
-
-    for copy in ops + zero + [zero_on(i, core) for i in range(2)]:
+    zero_take(0)
+    for a in range(2):
+        for q in range(2):
+            early_copy(a, q, q).wait_recv()
+        early_pass(a).start()
+    zero_rest(0)
+
+    @pl.loop(0, CHUNKS)
+    def _(step):
+        @pl.when(step + AHEAD < CHUNKS - 1)
+        def _():
+            forward(step + AHEAD)
+
+        compute(step)
+
+        @pl.when(step == 0)
+        def _():
+            zero_take(1)
+            zero_take(2)
+
+        @pl.when(step == 1)
+        def _():
+            zero_rest(1)
+            zero_rest(2)
+
+        @pl.when((step >= 1) & (step <= CHUNKS - LATE))
+        def _():
+            compute_own(step - 1)
+
+        @pl.when(step >= BEHIND)
+        def _():
+            finish(step - BEHIND)
+
+    pl.loop(CHUNKS - LATE, CHUNKS)(compute_own)
+    pl.loop(CHUNKS - BEHIND, CHUNKS)(finish)
+
+    for copy in ops:
         copy.wait_send()
-    for j in range(CHUNKS):
+    for i in range(3):
+        zero_copy(i).wait_send()
+        zero_on(i, core).wait_send()
+    for a in range(2):
+        for q in range(2):
+            early_copy(a, q, core).wait_send()
+
+    @pl.loop(0, CHUNKS)
+    def _(j):
         for q in range(2):
             for a in range(3):
                 near_copy(a, j, q, core).wait_send()
@@ -291,6 +375,7 @@
             pltpu.VMEM((n, 2, 1, width), jnp.float32),
             pltpu.VMEM((n, 2, rows, width), jnp.int16),
             pltpu.VMEM((n, 2, 1, width), jnp.float32),
+            pltpu.VMEM((2, 2 * rows, width), jnp.bfloat16),
             pltpu.SMEM(patterns.shape, jnp.int32),
             pltpu.SMEM(signs.shape, jnp.int32),
             dma((n,)), dma((5,)), dma((3,)),
@@ -300,7 +385,8 @@
             dma((n, 2, 2)), dma((n, 2, 2)),
             dma((n,)), dma((n,)),
             dma((5,)), dma((5,)),
-            dma((4,)), dma((4,)),
+            dma((6,)), dma((6,)),
+            dma((2, 2)), dma((2, 2)),
         ],
         compiler_params=pltpu.CompilerParams(
             collective_id=0, has_side_effects=True, vmem_limit_bytes=50 * 1024 * 1024

time: 46.3 us -> 45.9 us (level)
  no operation moved by 1% of the time
where the time goes in v3:
time: 45.9 us; the launch traced here: 45.8 us
  Pallas kernels  43.8 us (95%)
  local copies, waits for them, and re-layouts  1.32 us (3%)
  between operations  0.66 us (1%)
    pallas_call x1, Pallas kernels, per_device(): pl.pallas_call(kernel, out_shape=pltpu.VMEM((rows, rest), jnp.float32), i...  43.8 us
    unnamed x1, local copies, waits for them, and re-layouts  1.32 us

profile of v3, /device:TPU:1, one launch (start us, length us, event | category | flops | bytes accessed | tf_op | source)
XLA Modules:
  0.0 45.8 jit_solution(10246163890298430005)
XLA Ops:
  0.7 43.8 %shard_map.64 = f32[256,2048]{1,0:T(8,128)S(1)} custom-call(bf16[256,2048]{1,0:T(8,128)(2,1)} %bitcast.3, bf16[1024,256]{1,0:T(8,128)(2,1)} %h_imp.1, bf16[2,5,1024,256]{3,2,1,0:T(8,128)(2,1)} %hops.1, s32[2,5,8,8]{3,2,1,0:T(8,128)} %patterns_in.1, s32[5,1,8]{2,1,0:T(1,128)} %signs_in.1, f32[1]{0:T(128)S(6)} %copy.9.energy), custom_call_target="tpu_custom_call" | custom-call | tf_op jit(solution)/shard_map/pallas_call | solution.py:362
  44.5 1.3 %copy.8 = f32[1,256,2048]{2,1,0:T(8,128)} copy(f32[1,256,2048]{2,1,0:T(8,128)S(1)} %bitcast.2) | data formatting | bytes 4194304

commit v4 on v3

--- a/solution.py
+++ b/solution.py
@@ -10,7 +10,7 @@
 LEAST = 1e-30
 TOP = 32767.0
 AHEAD = 2
-BEHIND = 3
+BEHIND = 4
 LATE = 3
 LEFT = 128
 BLK = 128
@@ -75,22 +75,23 @@
     mats = [pltpu.make_async_copy(h_imp, weights.at[:, slot_rows(0, core)], mat_sem.at[0])]
     for level in range(1, 5):
         mats.append(pltpu.make_async_copy(hops.at[side[level], level], raw.at[level, core], mat_sem.at[level]))
-    for copy in small + mats + [whole]:
-        copy.start()
-
-    @pl.loop(0, CHUNKS)
-    def _(j):
-        own_copy(j).start()
-
     barrier = pltpu.get_barrier_semaphore()
     peers = [sibling] + across + near[0] + near[1] + near[2] + onward_both[0] + onward_both[1]
     for peer in peers:
         pl.semaphore_signal(barrier, inc=1, device_id=peer, device_id_type=MESH)
+    for copy in [whole] + small + mats:
+        copy.start()
+
+    @pl.loop(0, CHUNKS)
+    def _(j):
+        own_copy(j).start()
+
+    whole.wait()
     pl.semaphore_wait(barrier, len(peers))
 
     def near_copy(a, j, q, source):
         return remote(
-            psi.at[:, columns(q, j)],
+            local.at[:, columns(q, j)],
             amps.at[j, slot_rows(near_slot[a], source), :],
             near_send.at[a, j, q],
             near_recv.at[a, j, source],
@@ -103,7 +104,7 @@
 
     def pair_copy(j, source):
         return remote(
-            psi.at[:, columns(1 - core, j)],
+            local.at[:, columns(1 - core, j)],
             amps.at[j, slot_rows(0, source), :],
             pair_send.at[j],
             pair_recv.at[j],
@@ -132,7 +133,7 @@
 
     def early_copy(a, q, source):
         return remote(
-            psi.at[:, columns(q, CHUNKS - 1)],
+            local.at[:, columns(q, CHUNKS - 1)],
             early.at[a, pl.ds(pl.multiple_of(source * rows, rows), rows), :],
             early_send.at[a, q],
             early_recv.at[a, source],
@@ -288,7 +289,6 @@
         mask(level, level, 1 - core, z_lo, 0, 8)
     mats[0].wait()
     ops[0].wait_recv()
-    whole.wait()
     for j in range(1, AHEAD):
         forward(j)
     zero_take(0)
@@ -304,6 +304,10 @@
         def _():
             forward(step + AHEAD)
 
+        @pl.when(step >= BEHIND)
+        def _():
+            finish(step - BEHIND)
+
         compute(step)
 
         @pl.when(step == 0)
@@ -320,9 +324,6 @@
         def _():
             compute_own(step - 1)
 
-        @pl.when(step >= BEHIND)
-        def _():
-            finish(step - BEHIND)
 
     pl.loop(CHUNKS - LATE, CHUNKS)(compute_own)
     pl.loop(CHUNKS - BEHIND, CHUNKS)(finish)

time: 45.9 us -> 45.7 us (level)
  no operation moved by 1% of the time
where the time goes in v4:
time: 45.7 us; the launch traced here: 45.6 us
  Pallas kernels  43.6 us (95%)
  local copies, waits for them, and re-layouts  1.32 us (3%)
  between operations  0.66 us (1%)
    pallas_call x1, Pallas kernels, per_device(): pl.pallas_call(kernel, out_shape=pltpu.VMEM((rows, rest), jnp.float32), i...  43.6 us
    unnamed x1, local copies, waits for them, and re-layouts  1.32 us

profile of v4, /device:TPU:1, one launch (start us, length us, event | category | flops | bytes accessed | tf_op | source)
XLA Modules:
  0.0 45.6 jit_solution(7674135766697092224)
XLA Ops:
  0.7 43.6 %shard_map.64 = f32[256,2048]{1,0:T(8,128)S(1)} custom-call(bf16[256,2048]{1,0:T(8,128)(2,1)} %bitcast.3, bf16[1024,256]{1,0:T(8,128)(2,1)} %h_imp.1, bf16[2,5,1024,256]{3,2,1,0:T(8,128)(2,1)} %hops.1, s32[2,5,8,8]{3,2,1,0:T(8,128)} %patterns_in.1, s32[5,1,8]{2,1,0:T(1,128)} %signs_in.1, f32[1]{0:T(128)S(6)} %copy.9.energy), custom_call_target="tpu_custom_call" | custom-call | tf_op jit(solution)/shard_map/pallas_call | solution.py:363
  44.3 1.3 %copy.8 = f32[1,256,2048]{2,1,0:T(8,128)} copy(f32[1,256,2048]{2,1,0:T(8,128)S(1)} %bitcast.2) | data formatting | bytes 4194304

commit v5 on v4

--- a/solution.py
+++ b/solution.py
@@ -12,7 +12,7 @@
 AHEAD = 2
 BEHIND = 4
 LATE = 3
-LEFT = 128
+LEFT = 256
 BLK = 128
 
 

time: 45.7 us -> 45.7 us (level)
  no operation moved by 1% of the time
where the time goes in v5:
time: 45.7 us; the launch traced here: 45.6 us
  Pallas kernels  43.6 us (95%)
  local copies, waits for them, and re-layouts  1.32 us (3%)
  between operations  0.66 us (1%)
    pallas_call x1, Pallas kernels, per_device(): pl.pallas_call(kernel, out_shape=pltpu.VMEM((rows, rest), jnp.float32), i...  43.6 us
    unnamed x1, local copies, waits for them, and re-layouts  1.32 us

profile of v5, /device:TPU:1, one launch (start us, length us, event | category | flops | bytes accessed | tf_op | source)
XLA Modules:
  0.0 45.6 jit_solution(4280775228722082361)
XLA Ops:
  0.7 43.6 %shard_map.64 = f32[256,2048]{1,0:T(8,128)S(1)} custom-call(bf16[256,2048]{1,0:T(8,128)(2,1)} %bitcast.3, bf16[1024,256]{1,0:T(8,128)(2,1)} %h_imp.1, bf16[2,5,1024,256]{3,2,1,0:T(8,128)(2,1)} %hops.1, s32[2,5,8,8]{3,2,1,0:T(8,128)} %patterns_in.1, s32[5,1,8]{2,1,0:T(1,128)} %signs_in.1, f32[1]{0:T(128)S(6)} %copy.9.energy), custom_call_target="tpu_custom_call" | custom-call | tf_op jit(solution)/shard_map/pallas_call | solution.py:363
  44.2 1.3 %copy.8 = f32[1,256,2048]{2,1,0:T(8,128)} copy(f32[1,256,2048]{2,1,0:T(8,128)S(1)} %bitcast.2) | data formatting | bytes 4194304
